TPU v7x, 256 devices: a whole 4x4x8 slice. The times are simulated.
256 devices in a mesh: tile: 64 (over z, x, core), mem: 4 (over y).
Axes of the slice: x: 4, y: 4, z: 8, core: 2. Of those that a mesh axis runs over, the one named last changes fastest.
Arguments:
- footprints: bfloat16 [8192, 128, 128], P('tile'), may hold values from -0.1875 to 0.1875
- tile_row: int32 [8192], P('tile'), may hold values from 0 to 1023, as said below
- tile_col: int32 [8192], P('tile'), may hold values from 0 to 511, as said below
- prior_flux: bfloat16 [256, 65536], P('mem', 'tile'), may hold values from -12 to 12
- observed: float32 [256, 131072], P('mem', 'tile'), may hold values from -6 to 6
- precision_weight: int32 [131072], P('tile'), may hold values from 1 to 16
Outputs:
- gradient: float32 [256, 65536], P('mem', 'tile')
Inputs may be any that keep to these rules, and one draw needn't show every extreme that they name: Among the 128 tiles of each index of tile, at most 3 have a row block of one owner (owner = tile_row // 16); in every draw one owner gets exactly 3 from every index. Likewise with owner = tile_col // 8: at most 3 from one index of tile to one owner, and one owner gets exactly 3 from every index.
All inputs are finite; a program needn't handle non-finite values.
Results may differ from a plain program's by a relative error of at most 0.0052.
Values may be sent and summed in bfloat16 or wider, within the bound.
A program may use at most 64 MiB of HBM per device.

v0:
```python
import jax
import jax.numpy as jnp
from jax import lax
from jax.sharding import PartitionSpec as P

MEMBERS = 256
FLUX_DEV = 8
SOUND_DEV = 16


def sent_to_all(value, axis):
    size = lax.axis_size(axis)
    return lax.all_to_all(
        jnp.broadcast_to(value[None], (size, *value.shape)), axis, 0, 0, tiled=True
    )


def over_copies(value, axis):
    return sent_to_all(value, axis).sum(axis=0)


def slot_of(owners, capacity):
    entries = owners.shape[0]
    position = jnp.arange(entries)
    earlier = (owners[:, None] == owners[None, :]) & (position[None, :] < position[:, None])
    return owners * capacity + jnp.sum(earlier.astype(jnp.int32), axis=1)


def invert(slot_ids, slot_total):
    matches = slot_ids[None, :] == jnp.arange(slot_total)[:, None]
    sources = jnp.sum(jnp.where(matches, jnp.arange(slot_ids.shape[0])[None, :], 0), axis=1)
    return (sources, jnp.any(matches, axis=1))


def to_slots(values, sources, usage_flags):
    placed = jnp.take(values, sources, axis=1)
    return jnp.where(usage_flags[None, :, None], placed, jnp.zeros_like(placed))


def body(footprints, tile_row, tile_col, prior_flux, observed, precision_weight):
    devices_tile = lax.axis_size("tile")
    tile_count = footprints.shape[0]
    tile_size = footprints.shape[1]
    capacity = tile_count // devices_tile + max(1, tile_count // (2 * devices_tile))
    slot_total = devices_tile * capacity
    local_members = prior_flux.shape[0]
    local_sum = jnp.sum(prior_flux.astype(jnp.float32), axis=0)
    ensemble_sum = over_copies(local_sum, "mem")
    ensemble_mean = ensemble_sum / MEMBERS
    member_deviations = (prior_flux.astype(jnp.float32) - ensemble_mean[None, :]).astype(
        jnp.bfloat16
    )
    row_owner = tile_row // SOUND_DEV
    row_local = tile_row % SOUND_DEV
    col_owner = tile_col // FLUX_DEV
    col_local = tile_col % FLUX_DEV
    row_slot = slot_of(row_owner, capacity)
    col_slot = slot_of(col_owner, capacity)
    row_source, row_used = invert(row_slot, slot_total)
    col_source, col_used = invert(col_slot, slot_total)
    gathered = lax.all_gather(member_deviations, "tile", axis=1, tiled=True)
    retrieved_blocks = jnp.take(gathered.reshape(local_members, -1, tile_size), tile_col, axis=1)
    forward_terms = jnp.einsum(
        "mtk,trk->mtr", retrieved_blocks, footprints, preferred_element_type=jnp.float32
    )
    row_index = jnp.where(row_used, jnp.take(row_local, row_source), SOUND_DEV)
    sent_terms = to_slots(forward_terms, row_source, row_used)
    got_terms, got_rows = (
        lax.all_to_all(
            sent_terms.astype(jnp.bfloat16), "tile", split_axis=1, concat_axis=1, tiled=True
        ).astype(sent_terms.dtype),
        lax.all_to_all(row_index[None, :], "tile", split_axis=1, concat_axis=1, tiled=True),
    )
    got_rows = got_rows[0]
    row_match = (got_rows[None, :] == jnp.arange(SOUND_DEV)[:, None]).astype(jnp.float32)
    modelled = jnp.einsum("ds,msk->mdk", row_match, got_terms, precision=lax.Precision.HIGHEST)
    targets = observed.reshape(local_members, SOUND_DEV, tile_size)
    obs_weight = (precision_weight.astype(jnp.float32) / 8.0).reshape(SOUND_DEV, tile_size)
    weighted = (obs_weight[None, :, :] * (modelled - targets)).astype(jnp.bfloat16)
    reply_rows = jnp.take(weighted, jnp.minimum(got_rows, SOUND_DEV - 1), axis=1)
    returned = lax.all_to_all(reply_rows, "tile", split_axis=1, concat_axis=1, tiled=True)
    residual_tiles = jnp.take(returned, row_slot, axis=1)
    backward_terms = jnp.einsum(
        "mtr,trk->mtk", residual_tiles, footprints, preferred_element_type=jnp.float32
    )
    col_index = jnp.where(col_used, jnp.take(col_local, col_source), FLUX_DEV)
    sent_back = to_slots(backward_terms, col_source, col_used)
    got_back, got_cols = (
        lax.all_to_all(
            sent_back.astype(jnp.bfloat16), "tile", split_axis=1, concat_axis=1, tiled=True
        ).astype(sent_back.dtype),
        lax.all_to_all(col_index[None, :], "tile", split_axis=1, concat_axis=1, tiled=True),
    )
    col_match = (got_cols[0][None, :] == jnp.arange(FLUX_DEV)[:, None]).astype(jnp.float32)
    reduced_total = jnp.einsum("fs,msk->mfk", col_match, got_back, precision=lax.Precision.HIGHEST)
    gradient = reduced_total.reshape(local_members, FLUX_DEV * tile_size)
    return gradient


def solution(mesh):
    in_specs = (
        P("tile", None, None),
        P("tile"),
        P("tile"),
        P("mem", "tile"),
        P("mem", "tile"),
        P("tile"),
    )
    out_specs = P("mem", "tile")
    return jax.shard_map(body, mesh=mesh, in_specs=in_specs, out_specs=out_specs, check_vma=False)
```

profile of v0, /device:TPU:2, one launch (start us, length us, event | category | flops | bytes accessed | tf_op | source)
XLA Modules:
  0.0 407.8 jit_solution(12967651325447050244)
XLA Ops:
  6.5 0.9 convert_reduce_fusion
  7.5 9.6 %all_to_all.39 = f32[4,1,1024]{2,1,0:T(1,128)S(1)} all-to-all(f32[4,1,1024]{2,1,0:T(1,128)S(1)} %broadcast_in_dim.122), channel_id=1, replica_groups=mesh['tile'=64,'mem'=4] {'mem'}, dimensions={0} | all-to-all | bytes 32768 | tf_op jit(solution)/shard_map/all_to_all | solution.py:13
  17.2 1.6 fusion.26
  18.7 0.0 all-gather.2.cloned.1.call-update
  18.8 0.7 and_select_fusion.1
  19.4 0.2 convert_reduce_fusion.1
  19.6 0.1 select_reduce_fusion.1
  19.8 1.6 gather_fusion.3
  21.3 0.1 fusion.27
  21.5 0.7 all_to_all.25
  22.2 12.0 %all-to-all-start = ((s32[1,64,3]{2,0,1:T(1,128)}), s32[1,64,3]{2,0,1:T(1,128)S(1)}, u32[]{:S(2)}, u32[]{:S(2)}) async-start(s32[1,64,3]{2,0,1:T(1,128)} %bitcast), calls=%async_computation | async-start | bytes 65536 | tf_op jit(solution)/shard_map/all_to_all | solution.py:72
  34.2 0.7 and_select_fusion
  34.9 0.7 compare_and_fusion.2
  35.6 66.0 %all-gather.2.cloned.1.call-done = bf16[64,65536]{1,0:T(8,128)(2,1)} async-done(((bf16[64,1024]{1,0:T(8,128)(2,1)}), bf16[64,65536]{1,0:T(8,128)(2,1)}) %all-gather.2.cloned.1.call-update) | async-done | bytes 8388624 | tf_op jit(solution)/shard_map/all_gather | solution.py:61
  101.5 9.0 %copy_bitcast_fusion = bf16[64,512,128]{2,0,1:T(8,128)(2,1)} fusion(bf16[64,65536]{1,0:T(8,128)(2,1)} %all-gather.2.cloned.1.call-done), kind=kLoop, calls=%fused_computation.7 | loop fusion | bytes 16777216 | tf_op jit(solution)/shard_map/reshape | solution.py:62
  110.5 5.5 %gather_fusion = bf16[128,64,128]{2,1,0:T(8,128)(2,1)} fusion(bf16[64,512,128]{2,0,1:T(8,128)(2,1)} %copy_bitcast_fusion, s32[1024]{0:T(1024)S(1)} %pad_clamp_fusion.3), kind=kCustom, calls=%fused_computation.4 | custom fusion | bytes 4194816 | tf_op jit(solution)/shard_map/jit(_take)/gather | solution.py:62
  116.1 5.8 %convolution_bitcast_fusion.1 = bf16[64,128,128]{2,0,1:T(8,128)(2,1)S(1)} fusion(bf16[128,128,128]{2,1,0:T(8,128)(2,1)} %param.10, bf16[128,64,128]{2,1,0:T(8,128)(2,1)} %gather_fusion, pred[128]{0:T(512)(128)(4,1)S(1)} %compare_and_fusion.2), kind=kOutput, calls=%fused_computation.18 | convolution fusion | flops 269484032 | bytes 8388736 | tf_op jit(solution)/shard_map/mtk,trk->mtr/dot_general | solution.py:63
  121.8 2.7 gather_fusion.4
  124.6 4.3 %fusion.1 = bf16[64,192,128]{2,0,1:T(8,128)(2,1)} fusion(bf16[192,64,128]{2,1,0:T(8,128)(2,1)} %gather_fusion.4, pred[192]{0:T(512)(128)(4,1)S(1)} %get-tuple-element.14, pred[192]{0:T(512)(128)(4,1)S(1)} %fusion.27), kind=kLoop, calls=%fused_computation.11 | loop fusion | flops 3145728 | bytes 6291840 | tf_op jit(solution)/shard_map/convert_element_type | solution.py:70
  128.8 7.8 %all-to-all-start.2 = ((bf16[64,192,128]{2,0,1:T(8,128)(2,1)}), bf16[64,192,128]{2,0,1:T(8,128)(2,1)S(1)}, u32[]{:S(2)}, u32[]{:S(2)}) async-start(bf16[64,192,128]{2,0,1:T(8,128)(2,1)} %fusion.1), calls=%async_computation.2 | async-start | bytes 6291456 | tf_op jit(solution)/shard_map/all_to_all | solution.py:69
  136.7 1.9 copy.34
  138.6 0.5 broadcast.195
  139.1 0.7 minimum_reduce_fusion
  139.9 0.1 squeeze.3
  140.0 0.1 min.26
  140.2 70.2 %all-to-all-done.2 = bf16[64,192,128]{2,0,1:T(8,128)(2,1)S(1)} async-done(((bf16[64,192,128]{2,0,1:T(8,128)(2,1)}), bf16[64,192,128]{2,0,1:T(8,128)(2,1)S(1)}, u32[]{:S(2)}, u32[]{:S(2)}) %all-to-all-start.2) | async-done | bytes 3145760 | tf_op jit(solution)/shard_map/all_to_all | solution.py:69
  210.4 2.8 fusion.21
  213.3 0.1 copy.29
  213.3 1.2 gather_fusion.1
  214.5 2.1 select_bitcast_fusion
  216.6 5.4 %all-to-all-start.3 = ((bf16[64,192,128]{2,0,1:T(8,128)(2,1)}), bf16[64,192,128]{2,0,1:T(8,128)(2,1)S(1)}, u32[]{:S(2)}, u32[]{:S(2)}) async-start(bf16[64,192,128]{2,0,1:T(8,128)(2,1)} %select_bitcast_fusion), calls=%async_computation.3 | async-start | bytes 6291456 | tf_op jit(solution)/shard_map/all_to_all | solution.py:81
  222.0 0.2 convert_reduce_fusion.2
  222.2 0.1 select_reduce_fusion
  222.3 1.6 gather_fusion.6
  223.9 0.1 fusion.28
  224.0 0.8 all_to_all.31
  224.8 70.9 %all-to-all-done.3 = bf16[64,192,128]{2,0,1:T(8,128)(2,1)S(1)} async-done(((bf16[64,192,128]{2,0,1:T(8,128)(2,1)}), bf16[64,192,128]{2,0,1:T(8,128)(2,1)S(1)}, u32[]{:S(2)}, u32[]{:S(2)}) %all-to-all-start.3) | async-done | bytes 3145760 | tf_op jit(solution)/shard_map/all_to_all | solution.py:81
  295.8 5.4 %all-to-all-start.5 = ((s32[1,64,3]{2,0,1:T(1,128)}), s32[1,64,3]{2,0,1:T(1,128)S(1)}, u32[]{:S(2)}, u32[]{:S(2)}) async-start(s32[1,64,3]{2,0,1:T(1,128)} %bitcast.12), calls=%async_computation.5 | async-start | bytes 65536 | tf_op jit(solution)/shard_map/all_to_all | solution.py:92
  301.2 2.2 gather_fusion.2
  303.4 4.1 %convolution_bitcast_fusion = bf16[64,128,128]{2,0,1:T(8,128)(2,1)S(1)} fusion(bf16[128,128,128]{2,1,0:T(8,128)(2,1)} %param.10, bf16[128,64,128]{2,1,0:T(8,128)(2,1)} %gather_fusion.2, pred[128]{0:T(512)(128)(4,1)S(1)} %get-tuple-element.11), kind=kOutput, calls=%fused_computation.17 | convolution fusion | flops 269484032 | bytes 8388736 | tf_op jit(solution)/shard_map/mtr,trk->mtk/dot_general | solution.py:83
  307.5 2.7 gather_fusion.5
  310.2 4.3 %fusion = bf16[64,192,128]{2,0,1:T(8,128)(2,1)} fusion(bf16[192,64,128]{2,1,0:T(8,128)(2,1)} %gather_fusion.5, pred[192]{0:T(512)(128)(4,1)S(1)} %get-tuple-element.10, pred[192]{0:T(512)(128)(4,1)S(1)} %fusion.28), kind=kLoop, calls=%fused_computation.9 | loop fusion | flops 3145728 | bytes 6291840 | tf_op jit(solution)/shard_map/convert_element_type | solution.py:90
  314.5 10.3 %all-to-all-start.4 = ((bf16[64,192,128]{2,0,1:T(8,128)(2,1)}), bf16[64,192,128]{2,0,1:T(8,128)(2,1)S(1)}, u32[]{:S(2)}, u32[]{:S(2)}) async-start(bf16[64,192,128]{2,0,1:T(8,128)(2,1)} %fusion), calls=%async_computation.4 | async-start | bytes 6291456 | tf_op jit(solution)/shard_map/all_to_all | solution.py:89
  324.8 0.6 reduce.12
  325.4 0.1 eq.98
  325.5 73.0 %all-to-all-done.4 = bf16[64,192,128]{2,0,1:T(8,128)(2,1)S(1)} async-done(((bf16[64,192,128]{2,0,1:T(8,128)(2,1)}), bf16[64,192,128]{2,0,1:T(8,128)(2,1)S(1)}, u32[]{:S(2)}, u32[]{:S(2)}) %all-to-all-start.4) | async-done | bytes 3145760 | tf_op jit(solution)/shard_map/all_to_all | solution.py:89
  398.5 1.7 fusion.2
  400.2 0.8 copy.50
  (23 shorter events, 0.1 us)
Async XLA Ops:
  6.5 95.0 %all-gather.2.cloned.1.call-start = ((), (), s32[]{:S(2)}) async-start(), calls=%async_computation.6 | async-start | bytes 8519680 | tf_op jit(solution)/shard_map/all_gather | solution.py:61
  22.2 106.6 %all-to-all-start = ((s32[1,64,3]{2,0,1:T(1,128)}), s32[1,64,3]{2,0,1:T(1,128)S(1)}, u32[]{:S(2)}, u32[]{:S(2)}) async-start(s32[1,64,3]{2,0,1:T(1,128)} %bitcast), calls=%async_computation | async-start | bytes 65536 | tf_op jit(solution)/shard_map/all_to_all | solution.py:72
  128.8 9.8 %copy-start = (s32[2048]{0:T(1024)S(1)}, s32[2048]{0:T(1024)}, u32[]{:S(2)}) copy-start(s32[2048]{0:T(1024)} %param.15) | copy-start | bytes 24580
  128.8 81.6 %all-to-all-start.2 = ((bf16[64,192,128]{2,0,1:T(8,128)(2,1)}), bf16[64,192,128]{2,0,1:T(8,128)(2,1)S(1)}, u32[]{:S(2)}, u32[]{:S(2)}) async-start(bf16[64,192,128]{2,0,1:T(8,128)(2,1)} %fusion.1), calls=%async_computation.2 | async-start | bytes 6291456 | tf_op jit(solution)/shard_map/all_to_all | solution.py:69
  216.6 79.2 %all-to-all-start.3 = ((bf16[64,192,128]{2,0,1:T(8,128)(2,1)}), bf16[64,192,128]{2,0,1:T(8,128)(2,1)S(1)}, u32[]{:S(2)}, u32[]{:S(2)}) async-start(bf16[64,192,128]{2,0,1:T(8,128)(2,1)} %select_bitcast_fusion), calls=%async_computation.3 | async-start | bytes 6291456 | tf_op jit(solution)/shard_map/all_to_all | solution.py:81
  295.8 18.7 %all-to-all-start.5 = ((s32[1,64,3]{2,0,1:T(1,128)}), s32[1,64,3]{2,0,1:T(1,128)S(1)}, u32[]{:S(2)}, u32[]{:S(2)}) async-start(s32[1,64,3]{2,0,1:T(1,128)} %bitcast.12), calls=%async_computation.5 | async-start | bytes 65536 | tf_op jit(solution)/shard_map/all_to_all | solution.py:92
  314.5 84.0 %all-to-all-start.4 = ((bf16[64,192,128]{2,0,1:T(8,128)(2,1)}), bf16[64,192,128]{2,0,1:T(8,128)(2,1)S(1)}, u32[]{:S(2)}, u32[]{:S(2)}) async-start(bf16[64,192,128]{2,0,1:T(8,128)(2,1)} %fusion), calls=%async_computation.4 | async-start | bytes 6291456 | tf_op jit(solution)/shard_map/all_to_all | solution.py:89
Sparse Core Ops, SparseCore 0:
  18.9 82.6 all-gather.1
where the time goes:
time: 409 us; the launch traced here: 408 us
  waiting for transfers between devices  280 us (68%)
  starting transfers between devices  41 us (10%)
  local copies, waits for them, and re-layouts  31.6 us (8%)
  other arithmetic  17.4 us (4%)
  matrix products  14.4 us (4%)
  between operations  13.6 us (3%)
  blocking collectives  9.63 us (2%)
    all_to_all x1, waiting for transfers between devices, body(): lax.all_to_all(sent_back.astype(jnp.bfloat16), 'tile', split_axis=1, conc...  73 us
    all_to_all x1, waiting for transfers between devices, body(): lax.all_to_all(reply_rows, 'tile', split_axis=1, concat_axis=1, tiled=True)  70.9 us
    all_to_all x1, waiting for transfers between devices, body(): lax.all_to_all(sent_terms.astype(jnp.bfloat16), 'tile', split_axis=1, con...  70.2 us
    all_gather x1, waiting for transfers between devices, body(): gathered = lax.all_gather(member_deviations, 'tile', axis=1, tiled=True)  66 us
    all_to_all x1, starting transfers between devices, body(): lax.all_to_all(row_index[None, :], 'tile', split_axis=1, concat_axis=1, t...  12 us
    all_to_all x1, starting transfers between devices, body(): lax.all_to_all(sent_back.astype(jnp.bfloat16), 'tile', split_axis=1, conc...  10.3 us
    all_to_all x1, blocking collectives, sent_to_all(): lax.all_to_all(jnp.broadcast_to(value[None], (size, *value.shape)), axis,...  9.63 us
    reshape x1, local copies, waits for them, and re-layouts, body(): gathered.reshape(local_members, -1, tile_size)  9.01 us
  transfers between devices with their start and end apart: 6, of which 4 were waited for; matrix products, arithmetic and copies ran while one was open for 12% of the time, Pallas kernels for 0%

commit v1 on v0

--- a/solution.py
+++ b/solution.py
@@ -58,7 +58,11 @@
     col_slot = slot_of(col_owner, capacity)
     row_source, row_used = invert(row_slot, slot_total)
     col_source, col_used = invert(col_slot, slot_total)
-    gathered = lax.all_gather(member_deviations, "tile", axis=1, tiled=True)
+    count = lax.axis_size("tile")
+    repeats = [count if d == 1 else 1 for d in range(member_deviations.ndim)]
+    gathered = lax.all_to_all(
+        jnp.tile(member_deviations, repeats), "tile", split_axis=1, concat_axis=1, tiled=True
+    )
     retrieved_blocks = jnp.take(gathered.reshape(local_members, -1, tile_size), tile_col, axis=1)
     forward_terms = jnp.einsum(
         "mtk,trk->mtr", retrieved_blocks, footprints, preferred_element_type=jnp.float32

time: 409 us -> 551 us (1.35)
  waiting for transfers between devices: 280 us -> 396 us
  local copies, waits for them, and re-layouts: 31.6 us -> 63.5 us
  between operations: 13.6 us -> 0.27 us
  starting transfers between devices: 41 us -> 51.3 us
    all_to_all x0 -> x1, waiting for transfers between devices: none -> 182 us  [body(): lax.all_to_all(jnp.tile(member_deviations, repeats), 'tile', split_axis=1...]
    all_gather x1 -> x0, waiting for transfers between devices: 66 us -> none  [body(): gathered = lax.all_gather(member_deviations, 'tile', axis=1, tiled=True)]
    reshape x1 -> x2, local copies, waits for them, and re-layouts: 9.01 us -> 25.3 us  [body(): gathered.reshape(local_members, -1, tile_size)]
    all_to_all x0 -> x1, starting transfers between devices: none -> 12.3 us  [body(): lax.all_to_all(jnp.tile(member_deviations, repeats), 'tile', split_axis=1...]
    all_to_all x0 -> x1, local copies, waits for them, and re-layouts: none -> 11.3 us  [body(): lax.all_to_all(jnp.tile(member_deviations, repeats), 'tile', split_axis=1...]
  transfers between devices with their start and end apart: 6 -> 6, of which waited for: 4 -> 4; matrix products, arithmetic and copies ran while one was open for 12% -> 14% of each run, Pallas kernels for 0% -> 0%
where the time goes in v1:
time: 551 us; the launch traced here: 550 us
  waiting for transfers between devices  396 us (72%)
  local copies, waits for them, and re-layouts  63.5 us (12%)
  starting transfers between devices  51.3 us (9%)
  other arithmetic  14.8 us (3%)
  matrix products  14.4 us (3%)
  blocking collectives  9.63 us (2%)
    all_to_all x1, waiting for transfers between devices, body(): lax.all_to_all(jnp.tile(member_deviations, repeats), 'tile', split_axis=1...  182 us
    all_to_all x1, waiting for transfers between devices, body(): lax.all_to_all(sent_back.astype(jnp.bfloat16), 'tile', split_axis=1, conc...  73 us
    all_to_all x1, waiting for transfers between devices, body(): lax.all_to_all(reply_rows, 'tile', split_axis=1, concat_axis=1, tiled=True)  70.9 us
    all_to_all x1, waiting for transfers between devices, body(): lax.all_to_all(sent_terms.astype(jnp.bfloat16), 'tile', split_axis=1, con...  70.2 us
    reshape x2, local copies, waits for them, and re-layouts, body(): gathered.reshape(local_members, -1, tile_size)  25.3 us
    all_to_all x1, starting transfers between devices, body(): lax.all_to_all(jnp.tile(member_deviations, repeats), 'tile', split_axis=1...  12.3 us
    all_to_all x1, local copies, waits for them, and re-layouts, body(): lax.all_to_all(jnp.tile(member_deviations, repeats), 'tile', split_axis=1...  11.3 us
  transfers between devices with their start and end apart: 6, of which 4 were waited for; matrix products, arithmetic and copies ran while one was open for 14% of the time, Pallas kernels for 0%

profile of v1, /device:TPU:2, one launch (start us, length us, event | category | flops | bytes accessed | tf_op | source)
XLA Modules:
  0.0 550.3 jit_solution(1539384801928295491)
XLA Ops:
  0.0 0.9 convert_reduce_fusion
  1.0 9.6 %all_to_all.45 = f32[4,1,1024]{2,1,0:T(1,128)S(1)} all-to-all(f32[4,1,1024]{2,1,0:T(1,128)S(1)} %broadcast_in_dim.122), channel_id=1, replica_groups=mesh['tile'=64,'mem'=4] {'mem'}, dimensions={0} | all-to-all | bytes 32768 | tf_op jit(solution)/shard_map/all_to_all | solution.py:13
  10.6 0.9 fusion.26
  11.6 4.3 tile.2
  15.8 12.3 %all-to-all-start.2 = ((bf16[64,64,1024]{2,0,1:T(8,128)(2,1)}), bf16[64,64,1024]{2,0,1:T(8,128)(2,1)}, u32[]{:S(2)}, u32[]{:S(2)}) async-start(bf16[64,64,1024]{2,0,1:T(8,128)(2,1)} %tile.2), calls=%async_computation.2 | async-start | bytes 16777216 | tf_op jit(solution)/shard_map/all_to_all | solution.py:63
  28.2 0.2 convert_reduce_fusion.1
  28.4 0.1 select_reduce_fusion.1
  28.5 1.6 gather_fusion.3
  30.1 0.1 fusion.27
  30.2 0.8 all_to_all.29
  31.0 182.2 %all-to-all-done.2 = bf16[64,64,1024]{2,0,1:T(8,128)(2,1)} async-done(((bf16[64,64,1024]{2,0,1:T(8,128)(2,1)}), bf16[64,64,1024]{2,0,1:T(8,128)(2,1)}, u32[]{:S(2)}, u32[]{:S(2)}) %all-to-all-start.2) | async-done | bytes 8388640 | tf_op jit(solution)/shard_map/all_to_all | solution.py:63
  213.2 7.4 %all-to-all-start = ((s32[1,64,3]{2,0,1:T(1,128)}), s32[1,64,3]{2,0,1:T(1,128)S(1)}, u32[]{:S(2)}, u32[]{:S(2)}) async-start(s32[1,64,3]{2,0,1:T(1,128)} %bitcast), calls=%async_computation | async-start | bytes 65536 | tf_op jit(solution)/shard_map/all_to_all | solution.py:76
  220.6 11.3 %copy.29 = bf16[64,64,1024]{2,1,0:T(8,128)(2,1)} copy(bf16[64,64,1024]{2,0,1:T(8,128)(2,1)} %all-to-all-done.2) | data formatting | bytes 16777216 | tf_op jit(solution)/shard_map/all_to_all | solution.py:63
  231.9 13.3 %reshape.92 = bf16[64,512,128]{2,1,0:T(8,128)(2,1)} reshape(bf16[64,64,1024]{2,1,0:T(8,128)(2,1)} %copy.29) | data formatting | bytes 16777216 | tf_op jit(solution)/shard_map/reshape | solution.py:66
  245.2 12.0 %copy.30 = bf16[64,512,128]{2,0,1:T(8,128)(2,1)} copy(bf16[64,512,128]{2,1,0:T(8,128)(2,1)} %reshape.92) | data formatting | bytes 16777216 | tf_op jit(solution)/shard_map/reshape | solution.py:66
  257.2 5.5 %gather_fusion = bf16[128,64,128]{2,1,0:T(8,128)(2,1)} fusion(bf16[64,512,128]{2,0,1:T(8,128)(2,1)} %copy.30, s32[1024]{0:T(1024)S(1)} %pad_clamp_fusion.3), kind=kCustom, calls=%fused_computation.4 | custom fusion | bytes 4194816 | tf_op jit(solution)/shard_map/jit(_take)/gather | solution.py:66
  262.8 5.8 %convolution_bitcast_fusion.1 = bf16[64,128,128]{2,0,1:T(8,128)(2,1)S(1)} fusion(bf16[128,128,128]{2,1,0:T(8,128)(2,1)} %param.10, bf16[128,64,128]{2,1,0:T(8,128)(2,1)} %gather_fusion, pred[128]{0:T(512)(128)(4,1)S(1)} %compare_and_fusion.2), kind=kOutput, calls=%fused_computation.17 | convolution fusion | flops 269484032 | bytes 8388736 | tf_op jit(solution)/shard_map/mtk,trk->mtr/dot_general | solution.py:67
  268.5 2.7 gather_fusion.4
  271.2 4.3 fusion.1
  275.5 10.4 %all-to-all-start.3 = ((bf16[64,192,128]{2,0,1:T(8,128)(2,1)}), bf16[64,192,128]{2,0,1:T(8,128)(2,1)S(1)}, u32[]{:S(2)}, u32[]{:S(2)}) async-start(bf16[64,192,128]{2,0,1:T(8,128)(2,1)} %fusion.1), calls=%async_computation.3 | async-start | bytes 6291456 | tf_op jit(solution)/shard_map/all_to_all | solution.py:73
  286.0 1.9 copy.36
  287.9 0.5 broadcast.198
  288.4 0.7 minimum_reduce_fusion
  289.1 0.1 squeeze.3
  289.3 0.1 min.26
  289.5 70.2 %all-to-all-done.3 = bf16[64,192,128]{2,0,1:T(8,128)(2,1)S(1)} async-done(((bf16[64,192,128]{2,0,1:T(8,128)(2,1)}), bf16[64,192,128]{2,0,1:T(8,128)(2,1)S(1)}, u32[]{:S(2)}, u32[]{:S(2)}) %all-to-all-start.3) | async-done | bytes 3145760 | tf_op jit(solution)/shard_map/all_to_all | solution.py:73
  359.7 2.8 fusion.21
  362.5 0.1 copy.32
  362.6 1.2 gather_fusion.1
  363.8 2.1 select_bitcast_fusion
  365.8 5.4 all-to-all-start.4
  371.3 0.2 convert_reduce_fusion.2
  371.5 0.1 select_reduce_fusion
  371.6 1.6 gather_fusion.6
  373.2 0.1 fusion.28
  373.3 0.8 all_to_all.36
  374.1 70.9 %all-to-all-done.4 = bf16[64,192,128]{2,0,1:T(8,128)(2,1)S(1)} async-done(((bf16[64,192,128]{2,0,1:T(8,128)(2,1)}), bf16[64,192,128]{2,0,1:T(8,128)(2,1)S(1)}, u32[]{:S(2)}, u32[]{:S(2)}) %all-to-all-start.4) | async-done | bytes 3145760 | tf_op jit(solution)/shard_map/all_to_all | solution.py:85
  445.0 5.4 all-to-all-start.6
  450.5 2.2 gather_fusion.2
  452.6 4.1 convolution_bitcast_fusion
  456.7 2.7 gather_fusion.5
  459.5 4.3 fusion
  463.7 10.3 %all-to-all-start.5 = ((bf16[64,192,128]{2,0,1:T(8,128)(2,1)}), bf16[64,192,128]{2,0,1:T(8,128)(2,1)S(1)}, u32[]{:S(2)}, u32[]{:S(2)}) async-start(bf16[64,192,128]{2,0,1:T(8,128)(2,1)} %fusion), calls=%async_computation.5 | async-start | bytes 6291456 | tf_op jit(solution)/shard_map/all_to_all | solution.py:93
  474.0 0.6 reduce.12
  474.7 0.1 eq.98
  474.8 73.0 %all-to-all-done.5 = bf16[64,192,128]{2,0,1:T(8,128)(2,1)S(1)} async-done(((bf16[64,192,128]{2,0,1:T(8,128)(2,1)}), bf16[64,192,128]{2,0,1:T(8,128)(2,1)S(1)}, u32[]{:S(2)}, u32[]{:S(2)}) %all-to-all-start.5) | async-done | bytes 3145760 | tf_op jit(solution)/shard_map/all_to_all | solution.py:93
  547.8 1.7 fusion.2
  549.5 0.8 copy.51
  (29 shorter events, 0.2 us)
Async XLA Ops:
  15.8 12.4 %copy-start.2 = (s32[128]{0:T(128)S(1)}, s32[128]{0:T(128)}, u32[]{:S(2)}) copy-start(s32[128]{0:T(128)} %param.11) | copy-start | bytes 1540
  15.8 15.2 %copy-start.1 = (s32[128]{0:T(128)S(1)}, s32[128]{0:T(128)}, u32[]{:S(2)}) copy-start(s32[128]{0:T(128)} %param.12) | copy-start | bytes 1540
  15.8 197.4 %all-to-all-start.2 = ((bf16[64,64,1024]{2,0,1:T(8,128)(2,1)}), bf16[64,64,1024]{2,0,1:T(8,128)(2,1)}, u32[]{:S(2)}, u32[]{:S(2)}) async-start(bf16[64,64,1024]{2,0,1:T(8,128)(2,1)} %tile.2), calls=%async_computation.2 | async-start | bytes 16777216 | tf_op jit(solution)/shard_map/all_to_all | solution.py:63
  213.2 62.3 %all-to-all-start = ((s32[1,64,3]{2,0,1:T(1,128)}), s32[1,64,3]{2,0,1:T(1,128)S(1)}, u32[]{:S(2)}, u32[]{:S(2)}) async-start(s32[1,64,3]{2,0,1:T(1,128)} %bitcast), calls=%async_computation | async-start | bytes 65536 | tf_op jit(solution)/shard_map/all_to_all | solution.py:76
  275.5 12.4 %copy-start = (s32[2048]{0:T(1024)S(1)}, s32[2048]{0:T(1024)}, u32[]{:S(2)}) copy-start(s32[2048]{0:T(1024)} %param.15) | copy-start | bytes 24580
  275.5 84.2 %all-to-all-start.3 = ((bf16[64,192,128]{2,0,1:T(8,128)(2,1)}), bf16[64,192,128]{2,0,1:T(8,128)(2,1)S(1)}, u32[]{:S(2)}, u32[]{:S(2)}) async-start(bf16[64,192,128]{2,0,1:T(8,128)(2,1)} %fusion.1), calls=%async_computation.3 | async-start | bytes 6291456 | tf_op jit(solution)/shard_map/all_to_all | solution.py:73
  365.8 79.2 %all-to-all-start.4 = ((bf16[64,192,128]{2,0,1:T(8,128)(2,1)}), bf16[64,192,128]{2,0,1:T(8,128)(2,1)S(1)}, u32[]{:S(2)}, u32[]{:S(2)}) async-start(bf16[64,192,128]{2,0,1:T(8,128)(2,1)} %select_bitcast_fusion), calls=%async_computation.4 | async-start | bytes 6291456 | tf_op jit(solution)/shard_map/all_to_all | solution.py:85
  445.0 18.7 %all-to-all-start.6 = ((s32[1,64,3]{2,0,1:T(1,128)}), s32[1,64,3]{2,0,1:T(1,128)S(1)}, u32[]{:S(2)}, u32[]{:S(2)}) async-start(s32[1,64,3]{2,0,1:T(1,128)} %bitcast.12), calls=%async_computation.6 | async-start | bytes 65536 | tf_op jit(solution)/shard_map/all_to_all | solution.py:96
  463.7 84.0 %all-to-all-start.5 = ((bf16[64,192,128]{2,0,1:T(8,128)(2,1)}), bf16[64,192,128]{2,0,1:T(8,128)(2,1)S(1)}, u32[]{:S(2)}, u32[]{:S(2)}) async-start(bf16[64,192,128]{2,0,1:T(8,128)(2,1)} %fusion), calls=%async_computation.5 | async-start | bytes 6291456 | tf_op jit(solution)/shard_map/all_to_all | solution.py:93
